TPU v7x, 32 devices: a whole 2x2x4 slice. The times are simulated.
32 devices in a mesh: seq: 4 (over y, x), ep: 8 (over z, core).
Axes of the slice: x: 2, y: 2, z: 4, core: 2. Of those that a mesh axis runs over, the one named last changes fastest.
Arguments:
- tokens: bfloat16 [24, 576, 768], P('ep', 'seq'), may hold values from -6 to 6
- routes: int32 [24, 576, 2], P('ep', 'seq'), may hold values from 0 to 31, all different within a row
- priority: int32 [24, 576], P('ep', 'seq'), may hold values from 0 to 431, as said below
- hires: int32 [8], P('ep'), may hold values from 0 to 3
- gain_one: float32 [768], replicated, may hold values from 0.1 to 1.9
- shift_one: float32 [768], replicated, may hold values from -1.8 to 1.8
- w_qkv: bfloat16 [768, 2304], replicated, may hold values from -0.21875 to 0.21875
- w_proj: bfloat16 [768, 768], replicated, may hold values from -6 to 6
- gain_two: float32 [768], replicated, may hold values from 0.1 to 1.9
- shift_two: float32 [768], replicated, may hold values from -1.8 to 1.8
- w_router: bfloat16 [768, 32], replicated, may hold values from -0.15917969 to 0.15917969
- expert_in: bfloat16 [98304, 768], P('ep'), may hold values from -0.21875 to 0.21875
- expert_out: bfloat16 [98304, 768], P('ep'), may hold values from -2.5 to 2.5
- cotangent: bfloat16 [24, 576, 768], P('ep', 'seq'), may hold values from -6 to 6
Outputs:
- output: bfloat16 [24, 576, 768], P('ep', 'seq')
- input_grad: bfloat16 [24, 576, 768], P('ep', 'seq')
- gain_one_grad: float32 [768], replicated
- shift_one_grad: float32 [768], replicated
- qkv_grad: float32 [768, 2304], replicated
- proj_grad: float32 [768, 768], replicated
- gain_two_grad: float32 [768], replicated
- shift_two_grad: float32 [768], replicated
- router_grad: float32 [768, 32], replicated
- expert_in_grad: float32 [98304, 768], P('ep')
- expert_out_grad: float32 [98304, 768], P('ep')
- rms_stats: float32 [3], replicated
Inputs may be any that keep to these rules, and one draw needn't show every extreme that they name: `priority`: within each device block of 3 images times 144 positions, the priorities are a permutation of 0 to 431.
All inputs are finite; a program needn't handle non-finite values.
Results may differ from a plain program's by a relative error of at most 0.015.
Values may be sent and summed in bfloat16 or wider, within the bound.
No kernel may reach another device: no remote copies, remote signals or barrier semaphores. Data moves between devices by JAX's collectives and lax.ppermute only.
A program may use at most 320 MiB of HBM per device.

v0:
```python
import jax
import jax.numpy as jnp
from jax import lax
from jax.sharding import PartitionSpec as P

HEADS = 12
EXPERTS = 32
TOP = 2
PATCHES = 576
SHORT = 196
norm_eps = 1e-06
neg_big = -1e30


def norm_forward(values, norm_gain, norm_bias):
    row_mean = jnp.mean(values, axis=-1, keepdims=True)
    centred = values - row_mean
    inv_root = lax.rsqrt(jnp.mean(centred * centred, axis=-1, keepdims=True) + norm_eps)
    normed = centred * inv_root
    return (normed * norm_gain + norm_bias, normed, inv_root)


def norm_backward(grad_out, normed, inv_root, norm_gain):
    gain_grad = jnp.sum(grad_out * normed, axis=0)
    bias_grad = jnp.sum(grad_out, axis=0)
    scaled = grad_out * norm_gain
    grad_in = inv_root * (
        scaled
        - jnp.mean(scaled, axis=-1, keepdims=True)
        - normed * jnp.mean(scaled * normed, axis=-1, keepdims=True)
    )
    return (grad_in, gain_grad, bias_grad)


def gelu_slope(values):
    return (
        0.5 * (1.0 + lax.erf(values * 0.7071067811865476))
        + values * jnp.exp(-0.5 * values * values) * 0.3989422804014327
    )


def routing(route_rows, priority_rows, row_valid, capacity):
    row_total = route_rows.shape[0]
    by_priority = (
        jnp.zeros((row_total,), jnp.int32)
        .at[priority_rows]
        .set(jnp.arange(row_total, dtype=jnp.int32))
    )
    ordered = jnp.concatenate([route_rows[by_priority, route_rank] for route_rank in range(TOP)])
    ordered_valid = jnp.concatenate([row_valid[by_priority]] * TOP)
    expert_hits = (
        ordered[:, None] == jnp.arange(EXPERTS, dtype=jnp.int32)[None, :]
    ) & ordered_valid[:, None]
    running = jnp.cumsum(expert_hits.astype(jnp.int32), axis=0)
    ordered_slot = jnp.sum(jnp.where(expert_hits, running, 0), axis=1) - 1
    pair_slot = ordered_slot.reshape(TOP, row_total)[:, priority_rows].T
    is_kept = (pair_slot >= 0) & (pair_slot < capacity)
    return jnp.where(is_kept, route_rows * capacity + pair_slot, EXPERTS * capacity)


def slot_sources(slot_dest, fill_value, capacity, divisor):
    flat_dest = slot_dest.reshape(-1)
    source_ids = jnp.arange(flat_dest.shape[0], dtype=jnp.int32) // divisor
    table_ids = (
        jnp.full((EXPERTS * capacity + 1,), fill_value, jnp.int32).at[flat_dest].set(source_ids)
    )
    return table_ids[: EXPERTS * capacity]


def fan_out(slot_table, ep_count, split_count, local_experts, capacity):
    feature_width = slot_table.shape[-1]
    grouped = slot_table.reshape(ep_count // split_count, 1, local_experts, capacity, feature_width)
    spread = jnp.broadcast_to(
        grouped, (ep_count // split_count, split_count, local_experts, capacity, feature_width)
    )
    return spread.reshape(ep_count, local_experts, capacity, feature_width)


def fan_in(arrived, split_count):
    ep_count, local_experts, capacity, feature_width = arrived.shape
    grouped = arrived.reshape(
        ep_count // split_count, split_count, local_experts, capacity, feature_width
    )
    return jnp.sum(grouped.astype(jnp.float32), axis=1).reshape(-1, feature_width)


def score_block(query_heads, key_heads, key_mask, score_scale):
    raw_scores = (
        jnp.einsum("ishd,ithd->ihst", query_heads, key_heads, preferred_element_type=jnp.float32)
        * score_scale
    )
    return jnp.where(key_mask[:, None, None, :], raw_scores, neg_big)


def per_device(
    tokens,
    routes,
    priority,
    hires,
    gain_one,
    shift_one,
    w_qkv,
    w_proj,
    gain_two,
    shift_two,
    w_router,
    expert_in,
    expert_out,
    cotangent,
):
    image_count, patch_rows, model_width = tokens.shape
    row_count = image_count * patch_rows
    seq_count = lax.axis_size("seq")
    ep_count = lax.axis_size("ep")
    full_patches = patch_rows * seq_count
    head_width = model_width // HEADS
    score_scale = head_width ** (-0.5)
    local_experts = max(1, EXPERTS // ep_count)
    split_count = max(1, ep_count // EXPERTS)
    local_hidden = expert_in.shape[0] // local_experts
    capacity = max(2, (105 * TOP * row_count + 100 * EXPERTS - 1) // (100 * EXPERTS))
    seq_place = lax.axis_index("seq")

    def send_slots(slot_table):
        outgoing = fan_out(slot_table, ep_count, split_count, local_experts, capacity)
        return lax.all_to_all(outgoing, "ep", split_axis=0, concat_axis=0, tiled=True)

    def return_slots(part_rows):
        returned = lax.all_to_all(part_rows, "ep", split_axis=0, concat_axis=0, tiled=True)
        return fan_in(returned, split_count)

    image_length = jnp.where(jnp.arange(image_count, dtype=jnp.int32) < hires[0], PATCHES, SHORT)
    key_mask = jnp.arange(full_patches, dtype=jnp.int32)[None, :] < image_length[:, None]
    own_mask = (seq_place * patch_rows + jnp.arange(patch_rows, dtype=jnp.int32))[
        None, :
    ] < image_length[:, None]
    row_valid = own_mask.reshape(row_count)
    valid_col = row_valid.astype(jnp.float32)[:, None]
    inputs = tokens.reshape(row_count, model_width).astype(jnp.float32)
    head_shape = (image_count, -1, HEADS, head_width)
    first_out, normed_one, inv_one = norm_forward(inputs, gain_one, shift_one)
    attn_in = first_out.astype(jnp.bfloat16)
    packed = jnp.dot(attn_in, w_qkv, preferred_element_type=jnp.float32).astype(jnp.bfloat16)
    query_rows = packed[:, :model_width].reshape(image_count, patch_rows, model_width)
    key_rows = packed[:, model_width : 2 * model_width].reshape(
        image_count, patch_rows, model_width
    )
    value_rows = packed[:, 2 * model_width :].reshape(image_count, patch_rows, model_width)
    query_heads = query_rows.reshape(head_shape)
    keys_all, values_all = (
        lax.all_gather(key_rows, "seq", axis=1, tiled=True),
        lax.all_gather(value_rows, "seq", axis=1, tiled=True),
    )
    scores = score_block(query_heads, keys_all.reshape(head_shape), key_mask, score_scale)
    row_max = jnp.max(scores, axis=-1, keepdims=True)
    exp_scores = jnp.exp(scores - row_max)
    row_total = jnp.sum(exp_scores, axis=-1, keepdims=True)
    probs = exp_scores / row_total
    log_total = row_max + jnp.log(row_total)
    attended = (
        jnp.einsum(
            "ihst,ithd->ishd",
            probs.astype(jnp.bfloat16),
            values_all.reshape(head_shape),
            preferred_element_type=jnp.float32,
        )
        .reshape(row_count, model_width)
        .astype(jnp.bfloat16)
    )
    attn_out = jnp.dot(attended, w_proj, preferred_element_type=jnp.float32)
    middle = inputs + attn_out
    second_out, normed_two, inv_two = norm_forward(middle, gain_two, shift_two)
    moe_in = second_out.astype(jnp.bfloat16)
    logits = jnp.dot(moe_in, w_router, preferred_element_type=jnp.float32)
    gate_probs = jax.nn.softmax(logits, axis=-1)
    route_rows = routes.reshape(row_count, TOP)
    slot_dest = routing(route_rows, priority.reshape(row_count), row_valid, capacity)
    token_src = slot_sources(slot_dest, row_count, capacity, TOP)
    pair_src = slot_sources(slot_dest, row_count * TOP, capacity, 1)
    padded_in = jnp.concatenate([moe_in, jnp.zeros((1, model_width), jnp.bfloat16)], axis=0)
    arrived = send_slots(padded_in[token_src])
    w_first = expert_in.reshape(local_experts, local_hidden, model_width)
    w_second = expert_out.reshape(local_experts, local_hidden, model_width)
    pre_act = jnp.einsum("secd,efd->secf", arrived, w_first, preferred_element_type=jnp.float32)
    hidden = jax.nn.gelu(pre_act, approximate=False).astype(jnp.bfloat16)
    partial_out = jnp.einsum(
        "secf,efd->secd", hidden, w_second, preferred_element_type=jnp.float32
    ).astype(jnp.bfloat16)
    value_table = return_slots(partial_out)
    padded_values = jnp.concatenate([value_table, jnp.zeros((1, model_width), jnp.float32)], axis=0)
    pair_values = padded_values[slot_dest.reshape(-1)].reshape(row_count, TOP, model_width)
    chosen = jnp.take_along_axis(gate_probs, route_rows, axis=1)
    moe_out = jnp.sum(chosen[:, :, None] * pair_values, axis=1)
    total = middle + moe_out
    output = (total * valid_col).astype(jnp.bfloat16).reshape(image_count, patch_rows, model_width)
    stat_terms = jnp.stack(
        [
            jnp.sum(valid_col * attn_out * attn_out),
            jnp.sum(valid_col * moe_out * moe_out),
            jnp.sum(valid_col * total * total),
            jnp.sum(row_valid.astype(jnp.float32)) * model_width,
        ]
    )
    grad_total = cotangent.reshape(row_count, model_width).astype(jnp.float32) * valid_col
    grad_gate = jnp.sum(grad_total[:, None, :] * pair_values, axis=2)
    grad_value = (
        (grad_total[:, None, :] * chosen[:, :, None])
        .astype(jnp.bfloat16)
        .reshape(row_count * TOP, model_width)
    )
    padded_grad = jnp.concatenate([grad_value, jnp.zeros((1, model_width), jnp.bfloat16)], axis=0)
    grad_sent = send_slots(padded_grad[pair_src])
    grad_hidden = jnp.einsum(
        "secd,efd->secf", grad_sent, w_second, preferred_element_type=jnp.float32
    )
    grad_pre = (grad_hidden * gelu_slope(pre_act)).astype(jnp.bfloat16)
    rows_all = lax.all_gather(arrived, "seq", axis=0, tiled=True)
    sent_all = lax.all_gather(grad_sent, "seq", axis=0, tiled=True)
    pre_all = jnp.einsum("secd,efd->secf", rows_all, w_first, preferred_element_type=jnp.float32)
    hidden_all = jax.nn.gelu(pre_all, approximate=False).astype(jnp.bfloat16)
    grad_hidden_all = jnp.einsum(
        "secd,efd->secf", sent_all, w_second, preferred_element_type=jnp.float32
    )
    grad_pre_all = (grad_hidden_all * gelu_slope(pre_all)).astype(jnp.bfloat16)
    grad_second = jnp.einsum(
        "secf,secd->efd", hidden_all, sent_all, preferred_element_type=jnp.float32
    ).reshape(-1, model_width)
    grad_first = jnp.einsum(
        "secf,secd->efd", grad_pre_all, rows_all, preferred_element_type=jnp.float32
    ).reshape(-1, model_width)
    grad_part_in = jnp.einsum(
        "secf,efd->secd", grad_pre, w_first, preferred_element_type=jnp.float32
    ).astype(jnp.bfloat16)
    grad_in_table = return_slots(grad_part_in)
    padded_back = jnp.concatenate([grad_in_table, jnp.zeros((1, model_width), jnp.float32)], axis=0)
    grad_dispatch = jnp.sum(
        padded_back[slot_dest.reshape(-1)].reshape(row_count, TOP, model_width), axis=1
    )
    expert_ids = jnp.arange(EXPERTS, dtype=jnp.int32)
    grad_probs = jnp.sum(
        jnp.where(route_rows[:, :, None] == expert_ids[None, None, :], grad_gate[:, :, None], 0.0),
        axis=1,
    )
    grad_logits = (
        gate_probs * (grad_probs - jnp.sum(grad_probs * gate_probs, axis=-1, keepdims=True))
    ).astype(jnp.bfloat16)
    grad_router = jnp.einsum("rd,re->de", moe_in, grad_logits, preferred_element_type=jnp.float32)
    grad_moe_in = grad_dispatch + jnp.einsum(
        "re,de->rd", grad_logits, w_router, preferred_element_type=jnp.float32
    )
    grad_mid_norm, grad_gain_two, grad_shift_two = norm_backward(
        grad_moe_in, normed_two, inv_two, gain_two
    )
    grad_middle = grad_total + grad_mid_norm
    grad_attn = grad_middle.astype(jnp.bfloat16)
    grad_proj = jnp.einsum("rd,re->de", attended, grad_attn, preferred_element_type=jnp.float32)
    grad_attended = jnp.einsum(
        "re,de->rd", grad_attn, w_proj, preferred_element_type=jnp.float32
    ).astype(jnp.bfloat16)
    grad_heads = grad_attended.reshape(head_shape)
    keys_again, values_again = (
        lax.all_gather(key_rows, "seq", axis=1, tiled=True),
        lax.all_gather(value_rows, "seq", axis=1, tiled=True),
    )
    key_heads = keys_again.reshape(head_shape)
    value_heads = values_again.reshape(head_shape)
    probs_again = jnp.exp(score_block(query_heads, key_heads, key_mask, score_scale) - log_total)
    grad_probs_att = jnp.einsum(
        "ishd,ithd->ihst", grad_heads, value_heads, preferred_element_type=jnp.float32
    )
    delta = jnp.sum(grad_probs_att * probs_again, axis=-1, keepdims=True)
    grad_scores = (probs_again * (grad_probs_att - delta)).astype(jnp.bfloat16)
    grad_queries = (
        jnp.einsum("ihst,ithd->ishd", grad_scores, key_heads, preferred_element_type=jnp.float32)
        * score_scale
    )
    grad_keys_full = (
        jnp.einsum("ihst,ishd->ithd", grad_scores, query_heads, preferred_element_type=jnp.float32)
        * score_scale
    )
    grad_values_full = jnp.einsum(
        "ihst,ishd->ithd",
        probs_again.astype(jnp.bfloat16),
        grad_heads,
        preferred_element_type=jnp.float32,
    )
    grad_keys, grad_values = (
        lax.psum_scatter(
            grad_keys_full.reshape(image_count, full_patches, model_width),
            "seq",
            scatter_dimension=1,
            tiled=True,
        ),
        lax.psum_scatter(
            grad_values_full.reshape(image_count, full_patches, model_width),
            "seq",
            scatter_dimension=1,
            tiled=True,
        ),
    )
    grad_packed = jnp.concatenate(
        [
            grad_queries.reshape(row_count, model_width),
            grad_keys.reshape(row_count, model_width),
            grad_values.reshape(row_count, model_width),
        ],
        axis=1,
    ).astype(jnp.bfloat16)
    grad_qkv = jnp.einsum("rd,re->de", attn_in, grad_packed, preferred_element_type=jnp.float32)
    grad_attn_in = jnp.einsum("re,de->rd", grad_packed, w_qkv, preferred_element_type=jnp.float32)
    grad_in_norm, grad_gain_one, grad_shift_one = norm_backward(
        grad_attn_in, normed_one, inv_one, gain_one
    )
    input_grad = (
        (grad_middle + grad_in_norm)
        .astype(jnp.bfloat16)
        .reshape(image_count, patch_rows, model_width)
    )
    small = lax.psum(
        (grad_gain_one, grad_shift_one, grad_gain_two, grad_shift_two, stat_terms), ("seq", "ep")
    )
    big = lax.psum(
        tuple((g.astype(jnp.bfloat16) for g in (grad_qkv, grad_proj, grad_router))), ("seq", "ep")
    )
    summed = tuple((g.astype(jnp.float32) for g in big)) + small
    expert_grads = (grad_first, grad_second)
    rms_stats = jnp.sqrt(summed[7][:3] / summed[7][3])
    return (
        output,
        input_grad,
        summed[3],
        summed[4],
        summed[0],
        summed[1],
        summed[5],
        summed[6],
        summed[2],
        expert_grads[0],
        expert_grads[1],
        rms_stats,
    )


def solution(mesh):
    in_specs = (
        P("ep", "seq", None),
        P("ep", "seq", None),
        P("ep", "seq"),
        P("ep"),
        P(),
        P(),
        P(),
        P(),
        P(),
        P(),
        P(),
        P("ep", None),
        P("ep", None),
        P("ep", "seq", None),
    )
    out_specs = (
        P("ep", "seq", None),
        P("ep", "seq", None),
        P(),
        P(),
        P(),
        P(),
        P(),
        P(),
        P(),
        P("ep", None),
        P("ep", None),
        P(),
    )
    return jax.shard_map(
        per_device, mesh=mesh, in_specs=in_specs, out_specs=out_specs, check_vma=False
    )
```

profile of v0, /device:TPU:0, one launch (start us, length us, event | category | flops | bytes accessed | tf_op | source)
XLA Modules:
  0.0 815.0 jit_solution(9045719646256218311)
XLA Ops:
  15.6 3.3 reshape_reshape.9
  18.9 3.8 copy.141
  28.5 6.5 gather_fusion
  35.1 7.7 gather_fusion.1
  44.2 4.0 gather_fusion.2
  50.5 4.8 reduce-window.6
  65.3 5.5 scatter_custom_fusion.1
  71.6 5.4 copy.140
  76.9 5.0 fusion.167
  81.9 5.0 copy-done.1
  86.9 3.8 fusion.48
  90.7 9.3 %all-gather.5.cloned.1.call-done = bf16[3,576,768]{2,1,0:T(8,128)(2,1)} async-done(((bf16[3,144,768]{2,1,0:T(8,128)(2,1)}), bf16[3,576,768]{2,1,0:T(8,128)(2,1)}) %all-gather.5.cloned.1.call-update) | async-done | bytes 2654224 | tf_op jit(solution)/shard_map/all_gather | solution.py:152
  100.0 5.3 copy.139
  105.3 8.2 %fusion.72 = bf16[3,144,12,64]{1,3,2,0:T(8,128)(2,1)} fusion(bf16[3,576,12,64]{1,3,2,0:T(8,128)(2,1)} %bitcast.270, f32[3,12,144,576]{3,2,1,0:T(8,128)} %copy-done.1, f32[3,12,144]{2,1,0:T(8,128)} %fusion.48, f32[3,12,144]{2,1,0:T(8,128)} %copy-done.18), kind=kOutput, calls=%fused_computation.118 | convolution fusion | flops 391495680 | bytes 15303168 | tf_op jit(solution)/shard_map/ihst,ithd->ishd/dot_general | solution.py:161
  113.6 4.0 copy.142
  117.6 3.5 convert_element_type.134
  121.1 3.4 fusion.165
  128.0 6.7 gather_fusion.4
  137.1 3.7 copy.149
  140.8 5.1 all-to-all-start
  156.3 4.6 mul.305
  160.9 5.4 scatter_custom_fusion.2
  169.6 12.0 %gather_fusion.8 = f32[864]{0:T(1024)S(1)} fusion(f32[432,32]{0,1:T(8,128)} %fusion.83, s32[864]{0:T(1024)S(1)} %reshape.493), kind=kCustom, calls=%fused_computation.8 | custom fusion | bytes 13824 | tf_op jit(solution)/shard_map/jit(take_along_axis)/gather | solution.py:192
  184.8 7.0 gather_fusion.6
  194.3 3.6 copy.154
  197.9 5.1 all-to-all-start.2
  205.9 12.2 %fusion.63 = f32[4,8,29,3072]{3,2,1,0:T(8,128)} fusion(bf16[4,3072,768,1]{2,1,3,0:T(8,128)(2,1)} %bitcast.267, bf16[8,4,29,768]{3,1,2,0:T(4,128)(2,1)} %all-to-all-done), kind=kOutput, calls=%fused_computation.109 | convolution fusion | flops 4378853376 | bytes 31703040 | tf_op jit(solution)/shard_map/secd,efd->secf/dot_general | solution.py:184
  218.2 34.8 %fusion.69 = bf16[8,4,29,768]{3,2,0,1:T(8,128)(2,1)S(1)} fusion(bf16[4,3072,768,1]{2,1,3,0:T(8,128)(2,1)} %bitcast.283, f32[4,8,29,3072]{3,2,1,0:T(8,128)} %fusion.63), kind=kOutput, calls=%fused_computation.114 | convolution fusion | flops 4564869120 | bytes 31703040 | tf_op jit(solution)/shard_map/secf,efd->secd/dot_general | solution.py:186
  255.2 5.1 all-to-all-start.1
  263.2 20.4 %fusion.66 = bf16[8,4,29,768]{3,2,0,1:T(8,128)(2,1)} fusion(bf16[4,3072,768,1]{2,1,3,0:T(8,128)(2,1)} %bitcast.268, f32[4,8,29,3072]{3,2,1,0:T(8,128)} %fusion.63, bf16[4,3072,768,1]{2,1,3,0:T(8,128)(2,1)} %bitcast.284, bf16[8,4,29,768]{3,1,2,0:T(4,128)(2,1)} %all-to-all-done.2), kind=kOutput, calls=%fused_computation.113 | convolution fusion | flops 8786927616 | bytes 52002816 | tf_op jit(solution)/shard_map/secf,efd->secd/dot_general | solution.py:231
  283.5 3.7 copy.156
  287.2 7.8 all-to-all-done.1
  295.0 4.3 all-to-all-start.3
  305.1 3.2 copy.152
  310.8 3.1 pad_convert_fusion.1
  313.9 6.6 gather_fusion.5
  320.6 4.4 reshape.416
  325.0 7.5 multiply_reduce_fusion.1
  342.5 6.6 gather_fusion.7
  349.2 4.9 reshape.420
  354.0 6.0 reduce_sum.241
  362.8 5.3 fusion.76
  371.3 3.3 reshape.421
  374.6 3.8 copy.160
  378.4 14.9 %multiply_reduce_fusion = (f32[3,12,144]{2,1,0:T(8,128)S(1)}, f32[3,12,144,576]{3,2,1,0:T(8,128)}) fusion(f32[3,12,144,576]{3,2,1,0:T(8,128)} %copy-done.1, f32[3,12,144]{2,1,0:T(8,128)} %log_add_fusion, bf16[3,144,12,64]{1,3,2,0:T(8,128)(2,1)} %copy.160, bf16[3,576,12,64]{1,3,2,0:T(8,128)(2,1)} %bitcast.271), kind=kOutput, calls=%fused_computation.50 | convolution fusion | flops 391158720 | bytes 27247104 | tf_op jit(solution)/shard_map/ishd,ithd->ihst/dot_general | solution.py:268
  393.3 9.9 %multiply_convert_fusion = bf16[3,12,144,576]{3,2,1,0:T(8,128)(2,1)S(1)} fusion(f32[3,12,144,576]{3,2,1,0:T(8,128)} %get-tuple-element.53, f32[3,12,144,576]{3,2,1,0:T(8,128)} %copy-done.1, f32[3,12,144]{2,1,0:T(8,128)S(1)} %get-tuple-element.52, f32[3,12,144]{2,1,0:T(8,128)S(1)} %copy-done.15), kind=kLoop, calls=%fused_computation.49 | loop fusion | flops 11943936 | bytes 29901312 | tf_op jit(solution)/shard_map/convert_element_type | solution.py:272
  403.2 4.2 broadcast_multiply_fusion
  407.8 7.5 copy.163
  416.0 7.5 fusion.73
  423.6 4.0 copy.161
  427.5 3.5 reshape.422
  431.1 10.3 %fusion.50 = f32[3,12,64,576]{3,2,1,0:T(8,128)} fusion(bf16[3,144,12,64]{1,3,2,0:T(8,128)(2,1)} %copy.160, f32[3,12,144,576]{3,2,1,0:T(8,128)} %copy-done.1, f32[3,12,144]{2,1,0:T(8,128)} %log_add_fusion), kind=kOutput, calls=%fused_computation.89 | convolution fusion | flops 388177920 | bytes 17936640 | tf_op jit(solution)/shard_map/ihst,ishd->ithd/dot_general | solution.py:281
  441.4 7.5 copy.165
  450.8 40.8 %psum.62 = bf16[768,32]{0,1:T(8,128)(2,1)} all-reduce(bf16[768,32]{0,1:T(8,128)(2,1)} %convolution_convert_fusion.4), channel_id=1, replica_groups=mesh['seq'=4,'ep'=8] {'seq','ep'}, use_global_device_ids=true, to_apply=%region_36.37 | all-reduce | flops 24576 | bytes 98304 | tf_op jit(solution)/shard_map/psum | solution.py:322
  493.0 3.4 convolution_convert_fusion.2
  499.0 29.5 %fusion.169 = f32[4,32,29,3072]{3,1,2,0:T(8,128)} fusion(bf16[32,4,29,768]{3,0,2,1:T(8,128)(2,1)} %all-gather.11.cloned.1.call-done, bf16[4,3072,768,1]{2,1,3,0:T(8,128)(2,1)} %bitcast.269), kind=kOutput, calls=%fused_computation.287 | convolution fusion | flops 17515413504 | bytes 70189056 | tf_op jit(solution)/shard_map/secd,efd->secf/dot_general | solution.py:219
  528.4 117.1 %fusion.23 = f32[4,3072,768,1]{2,1,3,0:T(8,128)} fusion(bf16[32,4,29,768]{3,0,2,1:T(8,128)(2,1)} %all-gather.9.cloned.1.call-done, f32[4,32,29,3072]{3,1,2,0:T(8,128)} %fusion.169), kind=kOutput, calls=%fused_computation.46 | convolution fusion | flops 18256625664 | bytes 89063424 | tf_op jit(solution)/shard_map/secf,secd->efd/dot_general | solution.py:225
  650.0 5.3 convolution_convert_fusion
  655.4 53.0 %fusion.170 = f32[4,3072,768,1]{2,1,3,0:T(8,128)} fusion(bf16[32,4,29,768]{3,0,2,1:T(8,128)(2,1)} %all-gather.11.cloned.1.call-done, f32[4,32,29,3072]{3,1,2,0:T(8,128)} %fusion.169, bf16[32,4,29,768]{3,0,2,1:T(8,128)(2,1)} %all-gather.9.cloned.1.call-done, bf16[4,3072,768,1]{2,1,3,0:T(8,128)(2,1)} %bitcast.285), kind=kOutput, calls=%fused_computation.288 | convolution fusion | flops 35144859648 | bytes 113639424 | tf_op jit(solution)/shard_map/secf,secd->efd/dot_general | solution.py:228
  708.4 5.5 multiply_reduce_fusion.4
  713.9 41.6 %all-reduce.7 = (f32[768]{0:T(1024)}, f32[768]{0:T(1024)}, f32[768]{0:T(1024)}, f32[768]{0:T(1024)}, f32[4]{0:T(128)}) all-reduce(f32[768]{0:T(1024)} %get-tuple-element.17, f32[768]{0:T(1024)} %get-tuple-element.26, f32[768]{0:T(1024)S(1)} %copy-done.36, f32[768]{0:T(1024)S(1)} %copy-done.37, ...), channel_id=1, replica_groups=mesh['seq'=4,'ep'=8] {'seq','ep'}, use_global_device_ids=true, to_apply=%region_27.28 | all-reduce | flops 3076 | bytes 24608 | tf_op jit(solution)/shard_map/psum | solution.py:319
  759.8 3.2 add_convert_fusion
  763.1 37.7 %all-reduce.11.cloned.1.call-done = (bf16[768,2304]{1,0:T(8,128)(2,1)}, bf16[768,768]{1,0:T(8,128)(2,1)}) async-done(((bf16[768,2304]{1,0:T(8,128)(2,1)}, bf16[768,768]{1,0:T(8,128)(2,1)}), (bf16[768,2304]{1,0:T(8,128)(2,1)}, bf16[768,768]{1,0:T(8,128)(2,1)})) %all-reduce.11.cloned.1.call-update) | async-done | bytes 4718608 | tf_op jit(solution)/shard_map/psum | solution.py:322
  800.8 5.6 convert_element_type.154
  (205 shorter events, 102.3 us)
Async XLA Ops:
  7.2 4.6 copy-start
  7.2 64.4 %all-gather.7.cloned.1.call-start = ((), (), s32[]{:S(2)}) async-start(), calls=%async_computation.7 | async-start | bytes 3317760 | tf_op jit(solution)/shard_map/all_gather | solution.py:151
  10.2 1.5 copy-start.32
  10.3 1.5 copy-start.34
  11.8 3.1 copy-start.16
  13.5 10.4 %copy-start.31 = (s32[3,144,2]{1,2,0:T(2,128)S(1)}, s32[3,144,2]{1,2,0:T(2,128)}, u32[]{:S(2)}) copy-start(s32[3,144,2]{1,2,0:T(2,128)} %param.15) | copy-start | bytes 10372
  13.5 11.2 %copy-start.44 = (s32[3,144]{1,0:T(4,128)S(1)}, s32[3,144]{1,0:T(4,128)}, u32[]{:S(2)}) copy-start(s32[3,144]{1,0:T(4,128)} %param.16) | copy-start | bytes 5188
  14.9 85.1 %all-gather.5.cloned.1.call-start = ((), (), s32[]{:S(2)}) async-start(), calls=%async_computation.6 | async-start | bytes 3317760 | tf_op jit(solution)/shard_map/all_gather | solution.py:152
  24.9 0.6 copy-start.41
  49.0 6.3 copy-start.43
  65.3 5.5 copy-start.39
  81.9 5.0 copy-start.1
  81.9 5.0 copy-start.18
  113.6 12.1 %copy-start.24 = (f32[768]{0:T(1024)S(1)}, f32[768]{0:T(1024)}, u32[]{:S(2)}) copy-start(f32[768]{0:T(1024)} %param.22) | copy-start | bytes 9220
  113.6 12.1 %copy-start.42 = (f32[768]{0:T(1024)S(1)}, f32[768]{0:T(1024)}, u32[]{:S(2)}) copy-start(f32[768]{0:T(1024)} %param.23) | copy-start | bytes 9220
  124.5 1.2 copy-start.3
  124.5 1.4 copy-start.20
  125.6 0.6 copy-start.28
  126.2 0.9 copy-start.9
  140.8 57.1 %all-to-all-start = ((bf16[8,4,29,768]{3,1,2,0:T(4,128)(2,1)}), bf16[8,4,29,768]{3,1,2,0:T(4,128)(2,1)}, u32[]{:S(2)}, u32[]{:S(2)}) async-start(bf16[8,4,29,768]{3,1,2,0:T(4,128)(2,1)} %copy.149), calls=%async_computation | async-start | bytes 2850816 | tf_op jit(solution)/shard_map/all_to_all | solution.py:126
  146.6 21.2 %copy-start.26 = (f32[432]{0:T(512)}, f32[432]{0:T(512)S(1)}, u32[]{:S(2)}) copy-start(f32[432]{0:T(512)S(1)} %convert_element_type.139) | copy-start | bytes 5188
  152.8 1.0 copy-start.8
  167.8 0.6 copy-start.13
  167.8 0.6 copy-start.22
  168.4 0.6 copy-start.30
  169.6 12.0 %copy-start.38 = (s32[864]{0:T(1024)S(1)}, s32[864]{0:T(1024)}, u32[]{:S(2)}) copy-start(s32[864]{0:T(1024)} %reshape.418) | copy-start | bytes 10372
  181.7 10.2 %copy-start.5 = (f32[864]{0:T(1024)}, f32[864]{0:T(1024)S(1)}, u32[]{:S(2)}) copy-start(f32[864]{0:T(1024)S(1)} %gather_fusion.8) | copy-start | bytes 10372
  197.9 57.2 %all-to-all-start.2 = ((bf16[8,4,29,768]{3,1,2,0:T(4,128)(2,1)}), bf16[8,4,29,768]{3,1,2,0:T(4,128)(2,1)}, u32[]{:S(2)}, u32[]{:S(2)}) async-start(bf16[8,4,29,768]{3,1,2,0:T(4,128)(2,1)} %copy.154), calls=%async_computation.2 | async-start | bytes 2850816 | tf_op jit(solution)/shard_map/all_to_all | solution.py:126
  203.0 295.9 %all-gather.11.cloned.1.call-start = ((), (), s32[]{:S(2)}) async-start(), calls=%async_computation.11 | async-start | bytes 7127040 | tf_op jit(solution)/shard_map/all_gather | solution.py:217
  255.2 39.8 %all-to-all-start.1 = ((bf16[8,4,29,768]{3,1,2,0:T(4,128)(2,1)}), bf16[8,4,29,768]{3,1,2,0:T(4,128)(2,1)}, u32[]{:S(2)}, u32[]{:S(2)}) async-start(bf16[8,4,29,768]{3,1,2,0:T(4,128)(2,1)} %copy.151), calls=%async_computation.1 | async-start | bytes 2850816 | tf_op jit(solution)/shard_map/all_to_all | solution.py:129
  260.2 268.2 %all-gather.9.cloned.1.call-start = ((), (), s32[]{:S(2)}) async-start(), calls=%async_computation.10 | async-start | bytes 7127040 | tf_op jit(solution)/shard_map/all_gather | solution.py:218
  263.2 37.8 %copy-start.40 = (s32[864]{0:T(1024)S(1)}, s32[864]{0:T(1024)}, u32[]{:S(2)}) copy-start(s32[864]{0:T(1024)} %copy-done.39) | copy-start | bytes 10372
  263.2 37.8 %copy-start.6 = (f32[864]{0:T(1024)S(1)}, f32[864]{0:T(1024)}, u32[]{:S(2)}) copy-start(f32[864]{0:T(1024)} %copy-done.5) | copy-start | bytes 10372
  295.0 39.1 %all-to-all-start.3 = ((bf16[8,4,29,768]{3,1,2,0:T(4,128)(2,1)}), bf16[8,4,29,768]{3,1,2,0:T(4,128)(2,1)}, u32[]{:S(2)}, u32[]{:S(2)}) async-start(bf16[8,4,29,768]{3,1,2,0:T(4,128)(2,1)} %copy.156), calls=%async_computation.3 | async-start | bytes 2850816 | tf_op jit(solution)/shard_map/all_to_all | solution.py:129
  299.3 346.2 %reduce-scatter.3.cloned.1.call-start = ((), (), s32[]{:S(2)}) async-start(), calls=%async_computation.8 | async-start | bytes 6635520 | tf_op jit(solution)/shard_map/reduce_scatter | solution.py:288
  349.1 11.7 %copy-start.23 = (f32[432]{0:T(512)S(1)}, f32[432]{0:T(512)}, u32[]{:S(2)}) copy-start(f32[432]{0:T(512)} %copy-done.22) | copy-start | bytes 5188
  349.1 13.6 %copy-start.21 = (f32[432]{0:T(512)S(1)}, f32[432]{0:T(512)}, u32[]{:S(2)}) copy-start(f32[432]{0:T(512)} %copy-done.20) | copy-start | bytes 5188
  349.2 13.6 %copy-start.25 = (f32[768]{0:T(1024)S(1)}, f32[768]{0:T(1024)}, u32[]{:S(2)}) copy-start(f32[768]{0:T(1024)} %param.22) | copy-start | bytes 9220
  349.2 13.6 %copy-start.27 = (f32[432]{0:T(512)S(1)}, f32[432]{0:T(512)}, u32[]{:S(2)}) copy-start(f32[432]{0:T(512)} %copy-done.26) | copy-start | bytes 5188
  360.0 8.1 copy-start.4
  360.0 8.1 copy-start.12
  360.0 8.1 copy-start.29
  360.0 9.7 %copy-start.11 = (bf16[768,768]{1,0:T(8,128)(2,1)S(1)}, bf16[768,768]{1,0:T(8,128)(2,1)}, u32[]{:S(2)}) copy-start(bf16[768,768]{1,0:T(8,128)(2,1)} %param.21) | copy-start | bytes 3538948
  362.7 5.3 copy-start.19
  368.6 1.1 copy-start.7
  378.4 14.9 %copy-start.15 = (f32[3,12,144]{2,1,0:T(8,128)S(1)}, f32[3,12,144]{2,1,0:T(8,128)}, u32[]{:S(2)}) copy-start(f32[3,12,144]{2,1,0:T(8,128)} %log_add_fusion) | copy-start | bytes 62212
  393.3 9.9 %copy-start.10 = (bf16[3,144,12,64]{1,3,2,0:T(8,128)(2,1)S(1)}, bf16[3,144,12,64]{1,3,2,0:T(8,128)(2,1)}, u32[]{:S(2)}) copy-start(bf16[3,144,12,64]{1,3,2,0:T(8,128)(2,1)} %copy.141) | copy-start | bytes 1990660
  403.2 4.6 copy-start.2
  415.3 232.5 %reduce-scatter.5.cloned.1.call-start = ((), (), s32[]{:S(2)}) async-start(), calls=%async_computation.9 | async-start | bytes 6635520 | tf_op jit(solution)/shard_map/reduce_scatter | solution.py:294
  496.5 304.3 %all-reduce.11.cloned.1.call-start = ((), (), s32[]{:S(2)}) async-start(), calls=%async_computation.12 | async-start | bytes 9437184 | tf_op jit(solution)/shard_map/psum | solution.py:322
  649.2 0.8 copy-start.17
  655.4 53.0 %copy-start.33 = (f32[432]{0:T(512)S(1)}, f32[432]{0:T(512)}, u32[]{:S(2)}) copy-start(f32[432]{0:T(512)} %copy-done.32) | copy-start | bytes 5188
  655.4 53.0 %copy-start.35 = (f32[432]{0:T(512)S(1)}, f32[432]{0:T(512)}, u32[]{:S(2)}) copy-start(f32[432]{0:T(512)} %copy-done.34) | copy-start | bytes 5188
  708.4 5.5 copy-start.36
  708.4 5.5 copy-start.37
  800.8 5.6 copy-start.14
Sparse Core Ops, SparseCore 0:
  15.0 42.6 all-gather.6
  60.1 39.9 all-gather.4
  206.1 65.7 all-gather.10
  273.5 65.2 all-gather.8
  415.4 62.4 reduce-scatter.2
  496.6 62.5 reduce-scatter.4
  655.5 145.2 all-reduce.10
where the time goes:
time: 823 us; the launch traced here: 815 us
  matrix products  347 us (42%)
  local copies, waits for them, and re-layouts  210 us (26%)
  other arithmetic  84.3 us (10%)
  blocking collectives  82.4 us (10%)
  waiting for transfers between devices  55.6 us (7%)
  starting transfers between devices  20.2 us (2%)
  between operations  16.3 us (2%)
    dot_general x1, matrix products, per_device(): jnp.einsum('secf,secd->efd', hidden_all, sent_all, preferred_element_type...  117 us
    dot_general x1, matrix products, per_device(): jnp.einsum('secf,secd->efd', grad_pre_all, rows_all, preferred_element_ty...  53 us
    psum x1, blocking collectives, per_device(): lax.psum((grad_gain_one, grad_shift_one, grad_gain_two, grad_shift_two, s...  41.6 us
    psum x1, blocking collectives, per_device(): lax.psum(tuple((g.astype(jnp.bfloat16) for g in (grad_qkv, grad_proj, gra...  40.8 us
    psum x1, waiting for transfers between devices, per_device(): lax.psum(tuple((g.astype(jnp.bfloat16) for g in (grad_qkv, grad_proj, gra...  37.7 us
    dot_general x1, matrix products, per_device(): jnp.einsum('secf,efd->secd', hidden, w_second, preferred_element_type=jnp...  34.8 us
    dot_general x1, matrix products, per_device(): jnp.einsum('secd,efd->secf', rows_all, w_first, preferred_element_type=jn...  29.5 us
    dot_general x1, matrix products, per_device(): jnp.einsum('secf,efd->secd', grad_pre, w_first, preferred_element_type=jn...  20.4 us
  transfers between devices with their start and end apart: 11, of which 3 were waited for; matrix products, arithmetic and copies ran while one was open for 70% of the time, Pallas kernels for 0%

commit v1 on v0

--- a/solution.py
+++ b/solution.py
@@ -320,7 +320,8 @@
         (grad_gain_one, grad_shift_one, grad_gain_two, grad_shift_two, stat_terms), ("seq", "ep")
     )
     big = lax.psum(
-        tuple((g.astype(jnp.bfloat16) for g in (grad_qkv, grad_proj, grad_router))), ("seq", "ep")
+        lax.psum(tuple((g.astype(jnp.bfloat16) for g in (grad_qkv, grad_proj, grad_router))), "ep"),
+        "seq",
     )
     summed = tuple((g.astype(jnp.float32) for g in big)) + small
     expert_grads = (grad_first, grad_second)

time: 823 us -> 865 us (1.051)
  waiting for transfers between devices: 55.6 us -> 88.8 us
    all_gather x1, waiting for transfers between devices: 0.01 us -> 59.9 us  [per_device(): sent_all = lax.all_gather(grad_sent, 'seq', axis=0, tiled=True)]
    psum x1, waiting for transfers between devices: 37.7 us -> 0.01 us  [per_device(): lax.psum(tuple((g.astype(jnp.bfloat16) for g in (grad_qkv, grad_proj, gra...]
    psum x0 -> x1, blocking collectives: none -> 18.7 us  [per_device(): lax.psum(lax.psum(tuple((g.astype(jnp.bfloat16) for g in (grad_qkv, grad_...]
    psum x1, blocking collectives: 40.8 us -> 30.7 us  [per_device(): lax.psum(tuple((g.astype(jnp.bfloat16) for g in (grad_qkv, grad_proj, gra...]
  transfers between devices with their start and end apart: 11 -> 12, of which waited for: 3 -> 6; matrix products, arithmetic and copies ran while one was open for 70% -> 67% of each run, Pallas kernels for 0% -> 0%
where the time goes in v1:
time: 865 us; the launch traced here: 857 us
  matrix products  348 us (40%)
  local copies, waits for them, and re-layouts  209 us (24%)
  blocking collectives  89.8 us (10%)
  waiting for transfers between devices  88.8 us (10%)
  other arithmetic  84.5 us (10%)
  starting transfers between devices  20.3 us (2%)
  between operations  16.4 us (2%)
    dot_general x1, matrix products, per_device(): jnp.einsum('secf,secd->efd', hidden_all, sent_all, preferred_element_type...  117 us
    all_gather x1, waiting for transfers between devices, per_device(): sent_all = lax.all_gather(grad_sent, 'seq', axis=0, tiled=True)  59.9 us
    dot_general x1, matrix products, per_device(): jnp.einsum('secf,secd->efd', grad_pre_all, rows_all, preferred_element_ty...  53.5 us
    psum x1, blocking collectives, per_device(): lax.psum((grad_gain_one, grad_shift_one, grad_gain_two, grad_shift_two, s...  40.5 us
    dot_general x1, matrix products, per_device(): jnp.einsum('secf,efd->secd', hidden, w_second, preferred_element_type=jnp...  34.8 us
    psum x1, blocking collectives, per_device(): lax.psum(tuple((g.astype(jnp.bfloat16) for g in (grad_qkv, grad_proj, gra...  30.7 us
    dot_general x1, matrix products, per_device(): jnp.einsum('secd,efd->secf', rows_all, w_first, preferred_element_type=jn...  29.1 us
    dot_general x1, matrix products, per_device(): jnp.einsum('secf,efd->secd', grad_pre, w_first, preferred_element_type=jn...  21.8 us
  transfers between devices with their start and end apart: 12, of which 6 were waited for; matrix products, arithmetic and copies ran while one was open for 67% of the time, Pallas kernels for 0%

profile of v1, /device:TPU:0, one launch (start us, length us, event | category | flops | bytes accessed | tf_op | source)
XLA Modules:
  0.0 857.1 jit_solution(2918590233065473019)
XLA Ops:
  15.6 3.3 reshape_reshape.9
  18.9 3.8 copy.141
  28.5 6.5 gather_fusion
  35.0 7.7 gather_fusion.1
  44.1 4.0 gather_fusion.2
  50.4 4.8 reduce-window.6
  65.3 5.5 scatter_custom_fusion.1
  71.5 5.4 copy.140
  76.9 5.0 fusion.167
  81.9 5.0 copy-done.1
  86.9 3.8 fusion.48
  90.7 9.3 %all-gather.5.cloned.1.call-done = bf16[3,576,768]{2,1,0:T(8,128)(2,1)} async-done(((bf16[3,144,768]{2,1,0:T(8,128)(2,1)}), bf16[3,576,768]{2,1,0:T(8,128)(2,1)}) %all-gather.5.cloned.1.call-update) | async-done | bytes 2654224 | tf_op jit(solution)/shard_map/all_gather | solution.py:152
  100.0 5.3 copy.139
  105.3 8.2 fusion.72
  113.6 4.0 copy.142
  117.6 3.5 convert_element_type.134
  121.1 3.4 fusion.165
  127.9 6.7 gather_fusion.4
  137.0 3.7 copy.149
  140.7 5.1 all-to-all-start
  156.3 4.6 mul.305
  160.9 5.4 scatter_custom_fusion.2
  169.7 12.0 %gather_fusion.8 = f32[864]{0:T(1024)S(1)} fusion(f32[432,32]{0,1:T(8,128)} %fusion.83, s32[864]{0:T(1024)S(1)} %reshape.493), kind=kCustom, calls=%fused_computation.8 | custom fusion | bytes 13824 | tf_op jit(solution)/shard_map/jit(take_along_axis)/gather | solution.py:192
  184.9 7.0 gather_fusion.6
  194.3 3.7 copy.154
  198.0 5.1 all-to-all-start.2
  203.3 12.2 %fusion.63 = f32[4,8,29,3072]{3,2,1,0:T(8,128)} fusion(bf16[4,3072,768,1]{2,1,3,0:T(8,128)(2,1)} %bitcast.267, bf16[8,4,29,768]{3,1,2,0:T(4,128)(2,1)} %all-to-all-done), kind=kOutput, calls=%fused_computation.109 | convolution fusion | flops 4378853376 | bytes 31703040 | tf_op jit(solution)/shard_map/secd,efd->secf/dot_general | solution.py:184
  215.5 34.8 %fusion.69 = bf16[8,4,29,768]{3,2,0,1:T(8,128)(2,1)S(1)} fusion(bf16[4,3072,768,1]{2,1,3,0:T(8,128)(2,1)} %bitcast.283, f32[4,8,29,3072]{3,2,1,0:T(8,128)} %fusion.63), kind=kOutput, calls=%fused_computation.114 | convolution fusion | flops 4564869120 | bytes 31703040 | tf_op jit(solution)/shard_map/secf,efd->secd/dot_general | solution.py:186
  255.3 5.3 all-to-all-start.1
  260.7 21.8 %fusion.66 = bf16[8,4,29,768]{3,2,0,1:T(8,128)(2,1)} fusion(bf16[4,3072,768,1]{2,1,3,0:T(8,128)(2,1)} %bitcast.268, f32[4,8,29,3072]{3,2,1,0:T(8,128)} %fusion.63, bf16[4,3072,768,1]{2,1,3,0:T(8,128)(2,1)} %bitcast.284, bf16[8,4,29,768]{3,1,2,0:T(4,128)(2,1)} %all-to-all-done.2), kind=kOutput, calls=%fused_computation.113 | convolution fusion | flops 8786927616 | bytes 52002816 | tf_op jit(solution)/shard_map/secf,efd->secd/dot_general | solution.py:231
  282.5 3.7 copy.156
  286.2 9.2 %all-to-all-done.1 = bf16[8,4,29,768]{3,1,2,0:T(4,128)(2,1)} async-done(((bf16[8,4,29,768]{3,1,2,0:T(4,128)(2,1)}), bf16[8,4,29,768]{3,1,2,0:T(4,128)(2,1)}, u32[]{:S(2)}, u32[]{:S(2)}) %all-to-all-start.1) | async-done | bytes 1425440 | tf_op jit(solution)/shard_map/all_to_all | solution.py:129
  295.4 4.3 all-to-all-start.3
  313.9 6.6 gather_fusion.5
  320.5 4.4 reshape.416
  325.0 7.5 multiply_reduce_fusion.1
  342.8 6.6 gather_fusion.7
  349.4 4.9 reshape.420
  354.3 6.0 reduce_sum.241
  363.0 5.3 fusion.76
  371.5 3.3 reshape.421
  374.8 3.8 copy.160
  378.6 14.9 %multiply_reduce_fusion = (f32[3,12,144]{2,1,0:T(8,128)S(1)}, f32[3,12,144,576]{3,2,1,0:T(8,128)}) fusion(f32[3,12,144,576]{3,2,1,0:T(8,128)} %copy-done.1, f32[3,12,144]{2,1,0:T(8,128)} %log_add_fusion, bf16[3,144,12,64]{1,3,2,0:T(8,128)(2,1)} %copy.160, bf16[3,576,12,64]{1,3,2,0:T(8,128)(2,1)} %bitcast.271), kind=kOutput, calls=%fused_computation.50 | convolution fusion | flops 391158720 | bytes 27247104 | tf_op jit(solution)/shard_map/ishd,ithd->ihst/dot_general | solution.py:268
  393.5 9.9 %multiply_convert_fusion = bf16[3,12,144,576]{3,2,1,0:T(8,128)(2,1)S(1)} fusion(f32[3,12,144,576]{3,2,1,0:T(8,128)} %get-tuple-element.55, f32[3,12,144,576]{3,2,1,0:T(8,128)} %copy-done.1, f32[3,12,144]{2,1,0:T(8,128)S(1)} %get-tuple-element.54, f32[3,12,144]{2,1,0:T(8,128)S(1)} %copy-done.15), kind=kLoop, calls=%fused_computation.49 | loop fusion | flops 11943936 | bytes 29901312 | tf_op jit(solution)/shard_map/convert_element_type | solution.py:272
  403.4 4.2 broadcast_multiply_fusion
  408.0 7.5 copy.163
  415.6 9.9 %fusion.50 = f32[3,12,64,576]{3,2,1,0:T(8,128)} fusion(bf16[3,144,12,64]{1,3,2,0:T(8,128)(2,1)} %copy.160, f32[3,12,144,576]{3,2,1,0:T(8,128)} %copy-done.1, f32[3,12,144]{2,1,0:T(8,128)} %log_add_fusion), kind=kOutput, calls=%fused_computation.89 | convolution fusion | flops 388177920 | bytes 17936640 | tf_op jit(solution)/shard_map/ihst,ishd->ithd/dot_general | solution.py:281
  425.5 7.5 copy.165
  436.5 7.7 fusion.73
  444.2 4.0 copy.161
  448.2 3.5 reshape.422
  453.6 30.7 %psum.85 = bf16[768,32]{0,1:T(8,128)(2,1)} all-reduce(bf16[768,32]{0,1:T(8,128)(2,1)} %convolution_convert_fusion.4), channel_id=1, replica_groups=mesh['seq'=4,'ep'=8] {'ep'}, use_global_device_ids=true, to_apply=%region_38.39 | all-reduce | flops 24576 | bytes 98304 | tf_op jit(solution)/shard_map/psum | solution.py:323
  484.3 18.7 %psum.86 = bf16[768,32]{0,1:T(8,128)(2,1)} all-reduce(bf16[768,32]{0,1:T(8,128)(2,1)} %psum.85), channel_id=1, replica_groups=mesh['seq'=4,'ep'=8] {'seq'}, use_global_device_ids=true, to_apply=%region_39.40 | all-reduce | flops 24576 | bytes 98304 | tf_op jit(solution)/shard_map/psum | solution.py:322
  506.9 3.4 convolution_convert_fusion.2
  510.3 29.1 %fusion.169 = f32[4,32,29,3072]{3,1,2,0:T(8,128)} fusion(bf16[32,4,29,768]{3,0,2,1:T(8,128)(2,1)} %all-gather.11.cloned.1.call-done, bf16[4,3072,768,1]{2,1,3,0:T(8,128)(2,1)} %bitcast.269), kind=kOutput, calls=%fused_computation.287 | convolution fusion | flops 17515413504 | bytes 70189056 | tf_op jit(solution)/shard_map/secd,efd->secf/dot_general | solution.py:219
  546.3 5.3 convolution_convert_fusion
  551.6 59.9 %all-gather.9.cloned.1.call-done = bf16[32,4,29,768]{3,0,2,1:T(8,128)(2,1)} async-done(((bf16[8,4,29,768]{3,0,2,1:T(8,128)(2,1)}), bf16[32,4,29,768]{3,0,2,1:T(8,128)(2,1)}) %all-gather.9.cloned.1.call-update) | async-done | bytes 5701648 | tf_op jit(solution)/shard_map/all_gather | solution.py:218
  611.6 117.0 %fusion.23 = f32[4,3072,768,1]{2,1,3,0:T(8,128)} fusion(bf16[32,4,29,768]{3,0,2,1:T(8,128)(2,1)} %all-gather.9.cloned.1.call-done, f32[4,32,29,3072]{3,1,2,0:T(8,128)} %fusion.169), kind=kOutput, calls=%fused_computation.46 | convolution fusion | flops 18256625664 | bytes 89063424 | tf_op jit(solution)/shard_map/secf,secd->efd/dot_general | solution.py:225
  728.6 53.5 %fusion.170 = f32[4,3072,768,1]{2,1,3,0:T(8,128)} fusion(bf16[32,4,29,768]{3,0,2,1:T(8,128)(2,1)} %all-gather.11.cloned.1.call-done, f32[4,32,29,3072]{3,1,2,0:T(8,128)} %fusion.169, bf16[32,4,29,768]{3,0,2,1:T(8,128)(2,1)} %all-gather.9.cloned.1.call-done, bf16[4,3072,768,1]{2,1,3,0:T(8,128)(2,1)} %bitcast.285), kind=kOutput, calls=%fused_computation.288 | convolution fusion | flops 35144859648 | bytes 113639424 | tf_op jit(solution)/shard_map/secf,secd->efd/dot_general | solution.py:228
  782.1 5.6 multiply_reduce_fusion.4
  787.8 40.5 %all-reduce.7 = (f32[768]{0:T(1024)}, f32[768]{0:T(1024)}, f32[768]{0:T(1024)}, f32[768]{0:T(1024)}, f32[4]{0:T(128)}) all-reduce(f32[768]{0:T(1024)} %get-tuple-element.17, f32[768]{0:T(1024)} %get-tuple-element.26, f32[768]{0:T(1024)S(1)} %copy-done.36, f32[768]{0:T(1024)S(1)} %copy-done.37, ...), channel_id=1, replica_groups=mesh['seq'=4,'ep'=8] {'seq','ep'}, use_global_device_ids=true, to_apply=%region_27.28 | all-reduce | flops 3076 | bytes 24608 | tf_op jit(solution)/shard_map/psum | solution.py:319
  832.6 3.2 add_convert_fusion
  835.8 7.0 all-reduce.15.cloned.1.call-done
  842.8 5.6 convert_element_type.154
  (209 shorter events, 111.0 us)
Async XLA Ops:
  7.2 4.6 copy-start
  7.2 64.3 %all-gather.7.cloned.1.call-start = ((), (), s32[]{:S(2)}) async-start(), calls=%async_computation.7 | async-start | bytes 3317760 | tf_op jit(solution)/shard_map/all_gather | solution.py:151
  10.2 1.5 copy-start.32
  10.3 1.5 copy-start.34
  11.8 3.1 copy-start.16
  13.5 10.4 %copy-start.31 = (s32[3,144,2]{1,2,0:T(2,128)S(1)}, s32[3,144,2]{1,2,0:T(2,128)}, u32[]{:S(2)}) copy-start(s32[3,144,2]{1,2,0:T(2,128)} %param.15) | copy-start | bytes 10372
  13.5 11.2 %copy-start.44 = (s32[3,144]{1,0:T(4,128)S(1)}, s32[3,144]{1,0:T(4,128)}, u32[]{:S(2)}) copy-start(s32[3,144]{1,0:T(4,128)} %param.16) | copy-start | bytes 5188
  14.9 85.1 %all-gather.5.cloned.1.call-start = ((), (), s32[]{:S(2)}) async-start(), calls=%async_computation.6 | async-start | bytes 3317760 | tf_op jit(solution)/shard_map/all_gather | solution.py:152
  24.8 0.6 copy-start.41
  49.0 6.3 copy-start.43
  65.3 5.5 copy-start.39
  81.9 5.0 copy-start.1
  81.9 5.0 copy-start.18
  113.6 12.0 %copy-start.24 = (f32[768]{0:T(1024)S(1)}, f32[768]{0:T(1024)}, u32[]{:S(2)}) copy-start(f32[768]{0:T(1024)} %param.22) | copy-start | bytes 9220
  113.6 12.0 %copy-start.42 = (f32[768]{0:T(1024)S(1)}, f32[768]{0:T(1024)}, u32[]{:S(2)}) copy-start(f32[768]{0:T(1024)} %param.23) | copy-start | bytes 9220
  124.5 1.1 copy-start.3
  124.5 1.4 copy-start.20
  125.5 0.6 copy-start.28
  126.1 0.9 copy-start.9
  140.7 57.3 %all-to-all-start = ((bf16[8,4,29,768]{3,1,2,0:T(4,128)(2,1)}), bf16[8,4,29,768]{3,1,2,0:T(4,128)(2,1)}, u32[]{:S(2)}, u32[]{:S(2)}) async-start(bf16[8,4,29,768]{3,1,2,0:T(4,128)(2,1)} %copy.149), calls=%async_computation | async-start | bytes 2850816 | tf_op jit(solution)/shard_map/all_to_all | solution.py:126
  146.5 21.4 %copy-start.26 = (f32[432]{0:T(512)}, f32[432]{0:T(512)S(1)}, u32[]{:S(2)}) copy-start(f32[432]{0:T(512)S(1)} %convert_element_type.139) | copy-start | bytes 5188
  152.7 1.2 copy-start.8
  167.8 0.7 copy-start.13
  167.8 0.6 copy-start.22
  168.4 0.6 copy-start.30
  169.7 12.0 %copy-start.38 = (s32[864]{0:T(1024)S(1)}, s32[864]{0:T(1024)}, u32[]{:S(2)}) copy-start(s32[864]{0:T(1024)} %reshape.418) | copy-start | bytes 10372
  181.7 10.2 %copy-start.5 = (f32[864]{0:T(1024)}, f32[864]{0:T(1024)S(1)}, u32[]{:S(2)}) copy-start(f32[864]{0:T(1024)S(1)} %gather_fusion.8) | copy-start | bytes 10372
  198.0 57.3 %all-to-all-start.2 = ((bf16[8,4,29,768]{3,1,2,0:T(4,128)(2,1)}), bf16[8,4,29,768]{3,1,2,0:T(4,128)(2,1)}, u32[]{:S(2)}, u32[]{:S(2)}) async-start(bf16[8,4,29,768]{3,1,2,0:T(4,128)(2,1)} %copy.154), calls=%async_computation.2 | async-start | bytes 2850816 | tf_op jit(solution)/shard_map/all_to_all | solution.py:126
  203.1 307.2 %all-gather.11.cloned.1.call-start = ((), (), s32[]{:S(2)}) async-start(), calls=%async_computation.11 | async-start | bytes 7127040 | tf_op jit(solution)/shard_map/all_gather | solution.py:217
  255.3 40.1 %all-to-all-start.1 = ((bf16[8,4,29,768]{3,1,2,0:T(4,128)(2,1)}), bf16[8,4,29,768]{3,1,2,0:T(4,128)(2,1)}, u32[]{:S(2)}, u32[]{:S(2)}) async-start(bf16[8,4,29,768]{3,1,2,0:T(4,128)(2,1)} %copy.151), calls=%async_computation.1 | async-start | bytes 2850816 | tf_op jit(solution)/shard_map/all_to_all | solution.py:129
  260.7 40.7 %copy-start.40 = (s32[864]{0:T(1024)S(1)}, s32[864]{0:T(1024)}, u32[]{:S(2)}) copy-start(s32[864]{0:T(1024)} %copy-done.39) | copy-start | bytes 10372
  260.7 40.7 %copy-start.6 = (f32[864]{0:T(1024)S(1)}, f32[864]{0:T(1024)}, u32[]{:S(2)}) copy-start(f32[864]{0:T(1024)} %copy-done.5) | copy-start | bytes 10372
  295.4 39.0 %all-to-all-start.3 = ((bf16[8,4,29,768]{3,1,2,0:T(4,128)(2,1)}), bf16[8,4,29,768]{3,1,2,0:T(4,128)(2,1)}, u32[]{:S(2)}, u32[]{:S(2)}) async-start(bf16[8,4,29,768]{3,1,2,0:T(4,128)(2,1)} %copy.156), calls=%async_computation.3 | async-start | bytes 2850816 | tf_op jit(solution)/shard_map/all_to_all | solution.py:129
  299.7 239.7 %reduce-scatter.3.cloned.1.call-start = ((), (), s32[]{:S(2)}) async-start(), calls=%async_computation.8 | async-start | bytes 6635520 | tf_op jit(solution)/shard_map/reduce_scatter | solution.py:288
  349.4 11.7 %copy-start.23 = (f32[432]{0:T(512)S(1)}, f32[432]{0:T(512)}, u32[]{:S(2)}) copy-start(f32[432]{0:T(512)} %copy-done.22) | copy-start | bytes 5188
  349.4 13.6 %copy-start.21 = (f32[432]{0:T(512)S(1)}, f32[432]{0:T(512)}, u32[]{:S(2)}) copy-start(f32[432]{0:T(512)} %copy-done.20) | copy-start | bytes 5188
  349.4 13.6 %copy-start.25 = (f32[768]{0:T(1024)S(1)}, f32[768]{0:T(1024)}, u32[]{:S(2)}) copy-start(f32[768]{0:T(1024)} %param.22) | copy-start | bytes 9220
  349.4 13.6 %copy-start.27 = (f32[432]{0:T(512)S(1)}, f32[432]{0:T(512)}, u32[]{:S(2)}) copy-start(f32[432]{0:T(512)} %copy-done.26) | copy-start | bytes 5188
  360.2 8.1 copy-start.4
  360.2 8.1 copy-start.12
  360.2 8.1 copy-start.29
  360.2 9.7 %copy-start.11 = (bf16[768,768]{1,0:T(8,128)(2,1)S(1)}, bf16[768,768]{1,0:T(8,128)(2,1)}, u32[]{:S(2)}) copy-start(bf16[768,768]{1,0:T(8,128)(2,1)} %param.21) | copy-start | bytes 3538948
  363.0 5.3 copy-start.19
  368.9 1.1 copy-start.7
  378.6 14.9 %copy-start.15 = (f32[3,12,144]{2,1,0:T(8,128)S(1)}, f32[3,12,144]{2,1,0:T(8,128)}, u32[]{:S(2)}) copy-start(f32[3,12,144]{2,1,0:T(8,128)} %log_add_fusion) | copy-start | bytes 62212
  393.5 9.9 %copy-start.10 = (bf16[3,144,12,64]{1,3,2,0:T(8,128)(2,1)S(1)}, bf16[3,144,12,64]{1,3,2,0:T(8,128)(2,1)}, u32[]{:S(2)}) copy-start(bf16[3,144,12,64]{1,3,2,0:T(8,128)(2,1)} %copy.141) | copy-start | bytes 1990660
  403.4 4.6 copy-start.2
  415.5 128.5 %reduce-scatter.5.cloned.1.call-start = ((), (), s32[]{:S(2)}) async-start(), calls=%async_computation.9 | async-start | bytes 6635520 | tf_op jit(solution)/shard_map/reduce_scatter | solution.py:294
  433.0 178.6 %all-gather.9.cloned.1.call-start = ((), (), s32[]{:S(2)}) async-start(), calls=%async_computation.10 | async-start | bytes 7127040 | tf_op jit(solution)/shard_map/all_gather | solution.py:218
  435.8 292.8 %all-reduce.13.cloned.1.call-start = ((), (), s32[]{:S(2)}) async-start(), calls=%async_computation.12 | async-start | bytes 9437184 | tf_op jit(solution)/shard_map/psum | solution.py:323
  545.4 0.8 copy-start.17
  551.6 291.2 %all-reduce.15.cloned.1.call-start = ((), (), s32[]{:S(2)}) async-start(), calls=%async_computation.13 | async-start | bytes 9437184 | tf_op jit(solution)/shard_map/psum | solution.py:322
  728.6 53.5 %copy-start.33 = (f32[432]{0:T(512)S(1)}, f32[432]{0:T(512)}, u32[]{:S(2)}) copy-start(f32[432]{0:T(512)} %copy-done.32) | copy-start | bytes 5188
  728.6 53.5 %copy-start.35 = (f32[432]{0:T(512)S(1)}, f32[432]{0:T(512)}, u32[]{:S(2)}) copy-start(f32[432]{0:T(512)} %copy-done.34) | copy-start | bytes 5188
  782.1 5.7 copy-start.36
  782.1 5.6 copy-start.37
  842.8 5.6 copy-start.14
Sparse Core Ops, SparseCore 0:
  15.0 42.6 all-gather.6
  60.1 39.9 all-gather.4
  255.4 65.7 all-gather.10
  415.6 62.0 reduce-scatter.2
  481.2 62.7 reduce-scatter.4
  546.3 65.2 all-gather.8
  614.6 106.7 all-reduce.12
  728.7 113.9 all-reduce.14
